TPU v7x, 512 devices: a whole 4x4x16 slice. The times are simulated.
512 devices in a mesh: freq: 64 (over z, x_hi, core), space: 8 (over x_lo, y).
Axes of the slice: x: 4 (x_hi: 2, x_lo: 2; x = x_hi * 2 + x_lo), y: 4, z: 16, core: 2. Of those that a mesh axis runs over, the one named last changes fastest.
Arguments:
- series: bfloat16 [2048, 131072], P('freq', 'space')
- starts: int32 [7], replicated, may hold values from 0 to 1536, as said below
- freqs: int32 [64], replicated, may hold values from 0 to 511, as said below
- alpha: int32 [1], replicated, may hold values from 1 to 63
Outputs:
- spectra: bfloat16 [64, 2, 7, 131072], P('freq', None, None, 'space')
- gram: float32 [64, 2, 63, 63], P('freq')
Inputs may be any that keep to these rules, and one draw needn't show every extreme that they name: `starts`: increasing; the first is 0, the last 1536; consecutive ones lie 512 / 4 to 384 apart. `freqs`: 64 distinct bins, 0 and 511 among them.
All inputs are finite; a program needn't handle non-finite values.
Results may differ from a plain program's by a relative error of at most 0.005.
Values may be sent and summed in bfloat16 or wider, within the bound.
No kernel may reach another device: no remote copies, remote signals or barrier semaphores. Data moves between devices by JAX's collectives and lax.ppermute only.
A program may use at most 64 MiB of HBM per device.

v0:
```python
import math
import jax
import jax.numpy as jnp
from jax import lax
from jax.sharding import PartitionSpec as P

NFFT = 512
NBLK = 7
HALF = 4
SHIFTS = 9


def transform_table(freqs, alpha):
    sample_index = jnp.arange(NFFT, dtype=jnp.int32)
    shift_index = jnp.arange(SHIFTS, dtype=jnp.int32) - HALF
    freq_bins = jnp.mod(freqs[:, None] + shift_index[None, :] * alpha[0], NFFT)
    phase_steps = jnp.mod(freq_bins[:, :, None] * sample_index[None, None, :], NFFT)
    phase = phase_steps.astype(jnp.float32) * (2.0 * math.pi / NFFT)
    sample_float = sample_index.astype(jnp.float32)
    window_shape = 0.5 - 0.5 * jnp.cos(sample_float * (2.0 * math.pi / NFFT))
    window_scale = window_shape / jnp.sqrt(jnp.sum(window_shape * window_shape))
    real_part = window_scale * jnp.cos(phase)
    imag_part = -(window_scale * jnp.sin(phase))
    return jnp.stack([real_part, imag_part], axis=1).astype(jnp.bfloat16)


def split_quadrants(products, order):
    real_gram = products[..., :order, :order] + products[..., order:, order:]
    imag_gram = products[..., :order, order:] - products[..., order:, :order]
    return jnp.stack([real_gram, imag_gram], axis=-3)


def per_device(series, starts, freqs, alpha):
    slab_cells = series.shape[1]
    total_cells = slab_cells * lax.axis_size("space")
    nfreq = freqs.shape[0]
    order = SHIFTS * NBLK
    local_rows = lax.all_to_all(series, "freq", split_axis=1, concat_axis=0, tiled=True)
    local_cells = local_rows.shape[1]
    flat_table = transform_table(freqs, alpha).reshape(nfreq * 2 * SHIFTS, NFFT)
    blocks = []
    for block in range(NBLK):
        block_rows = lax.dynamic_slice_in_dim(local_rows, starts[block], NFFT, 0)
        spec_block = jnp.dot(flat_table, block_rows, preferred_element_type=jnp.float32)
        blocks.append(spec_block.astype(jnp.bfloat16).reshape(nfreq, 2, SHIFTS, local_cells))
    blockspec = jnp.stack(blocks, axis=3)
    received = lax.all_to_all(blockspec, "freq", split_axis=0, concat_axis=4, tiled=True)
    stacked = received.reshape(2 * order, slab_cells)
    products = lax.dot_general(
        stacked, stacked, (((1,), (1,)), ((), ())), preferred_element_type=jnp.float32
    )
    gram_part = split_quadrants(products, order)[None]
    own_spectra = received[:, :, HALF]
    gram = lax.psum(gram_part, "space") / total_cells
    return (own_spectra, gram)


def solution(mesh):
    placed = (P("freq", "space"), P(), P(), P())
    return jax.shard_map(
        per_device,
        mesh=mesh,
        in_specs=placed,
        out_specs=(P("freq", None, None, "space"), P("freq", None, None, None)),
        check_vma=False,
    )
```

profile of v0, /device:TPU:4, one launch (start us, length us, event | category | flops | bytes accessed | tf_op | source)
XLA Modules:
  0.0 362.7 jit_solution(13131280645304690328)
XLA Ops:
  0.6 2.3 copy.29
  3.0 18.9 %all-to-all-start = ((bf16[32,64,256]{2,0,1:T(8,128)(2,1)}), bf16[32,64,256]{2,0,1:T(8,128)(2,1)}, u32[]{:S(2)}, u32[]{:S(2)}) async-start(bf16[32,64,256]{2,0,1:T(8,128)(2,1)} %bitcast.40), calls=%async_computation | async-start | bytes 2097152 | tf_op jit(solution)/shard_map/all_to_all | solution.py:38
  33.3 5.4 %multiply_convert_fusion = (bf16[64,1,9,512]{3,0,2,1:T(8,128)(2,1)S(1)}, bf16[64,1,9,512]{3,0,2,1:T(8,128)(2,1)S(1)}) fusion(s32[64,9]{0,1:T(8,128)S(1)} %add_select_fusion.2, f32[512]{0:T(512)S(1)} %fusion.16), kind=kLoop, calls=%fused_computation.15 | loop fusion | flops 5603328 | bytes 1184000 | tf_op jit(solution)/shard_map/convert
  44.5 33.4 %all-to-all-done = bf16[32,64,256]{2,0,1:T(8,128)(2,1)} async-done(((bf16[32,64,256]{2,0,1:T(8,128)(2,1)}), bf16[32,64,256]{2,0,1:T(8,128)(2,1)}, u32[]{:S(2)}, u32[]{:S(2)}) %all-to-all-start) | async-done | bytes 1048608 | tf_op jit(solution)/shard_map/all_to_all | solution.py:38
  77.9 1.5 convolution_convert_fusion.6
  80.6 1.5 convolution_convert_fusion.5
  82.3 2.3 convolution_convert_fusion.4
  84.7 1.3 stack_reshape.23
  86.0 2.3 convolution_convert_fusion.3
  88.3 2.2 stack_reshape.24
  90.5 2.3 convolution_convert_fusion.2
  92.8 2.1 stack_reshape.25
  94.9 2.3 convolution_convert_fusion.1
  97.2 2.1 stack_reshape.26
  99.3 2.3 convolution_convert_fusion
  101.6 1.3 stack_reshape.27
  102.9 1.1 constant_dynamic-update-slice_fusion.5
  110.9 8.5 %copy.21 = bf16[64,2,9,7,256]{4,1,3,2,0:T(2,128)(2,1)} copy(bf16[64,2,9,7,256]{4,2,1,0,3:T(8,128)(2,1)} %constant_dynamic-update-slice_fusion) | data formatting | bytes 8257536 | tf_op jit(solution)/shard_map/stack | solution.py:46
  119.4 193.4 %all_to_all.37 = bf16[64,2,9,7,256]{4,1,3,2,0:T(2,128)(2,1)S(1)} all-to-all(bf16[64,2,9,7,256]{4,1,3,2,0:T(2,128)(2,1)} %copy.21), channel_id=1, replica_groups=mesh['freq'=64,'space'=8] {'freq'}, dimensions={0} | all-to-all | bytes 8257536 | tf_op jit(solution)/shard_map/all_to_all | solution.py:47
  315.3 2.9 copy.27
  318.2 1.2 fusion.25
  319.6 34.6 %psum.7 = f32[1,2,63,63]{3,2,1,0:T(8,128)S(1)} all-reduce(f32[1,2,63,63]{3,2,1,0:T(8,128)S(1)} %maximum_bitcast_fusion), channel_id=1, replica_groups=mesh['freq'=64,'space'=8] {'space'}, use_global_device_ids=true, to_apply=%region_1.2 | all-reduce | flops 7938 | bytes 63504 | tf_op jit(solution)/shard_map/psum | solution.py:54
  354.9 6.7 %copy.26 = bf16[1,64,9,7,1,2,256]{6,5,1,4,3,2,0:T(2,128)(2,1)S(1)} copy(bf16[1,64,9,7,1,2,256]{6,5,4,3,2,1,0:T(2,128)(2,1)} %bitcast.44) | data formatting | bytes 8257536 | tf_op jit(solution)/shard_map/all_to_all | solution.py:47
  361.6 1.1 slice_bitcast_fusion
  (34 shorter events, 14.6 us)
Async XLA Ops:
  3.0 18.9 %copy-start.4 = (s32[7]{0:T(128)S(1)}, s32[7]{0:T(128)}, u32[]{:S(2)}) copy-start(s32[7]{0:T(128)} %param.5) | copy-start | bytes 88
  3.0 30.3 %copy-start.5 = (s32[64]{0:T(128)S(1)}, s32[64]{0:T(128)}, u32[]{:S(2)}) copy-start(s32[64]{0:T(128)} %param.6) | copy-start | bytes 772
  3.0 74.9 %all-to-all-start = ((bf16[32,64,256]{2,0,1:T(8,128)(2,1)}), bf16[32,64,256]{2,0,1:T(8,128)(2,1)}, u32[]{:S(2)}, u32[]{:S(2)}) async-start(bf16[32,64,256]{2,0,1:T(8,128)(2,1)} %bitcast.40), calls=%async_computation | async-start | bytes 2097152 | tf_op jit(solution)/shard_map/all_to_all | solution.py:38
  104.0 1.6 copy-start.1
  105.6 1.6 copy-start.2
  107.2 1.6 copy-start.3
  312.8 1.9 copy-start
where the time goes:
time: 364 us; the launch traced here: 363 us
  blocking collectives  228 us (63%)
  local copies, waits for them, and re-layouts  45.3 us (12%)
  waiting for transfers between devices  33.4 us (9%)
  starting transfers between devices  18.9 us (5%)
  matrix products  15.6 us (4%)
  between operations  15.1 us (4%)
  other arithmetic  6.35 us (2%)
    all_to_all x1, blocking collectives, per_device(): lax.all_to_all(blockspec, 'freq', split_axis=0, concat_axis=4, tiled=True)  193 us
    psum x1, blocking collectives, per_device(): gram = lax.psum(gram_part, 'space') / total_cells  34.6 us
    all_to_all x1, waiting for transfers between devices, per_device(): lax.all_to_all(series, 'freq', split_axis=1, concat_axis=0, tiled=True)  33.4 us
    another operation x9, local copies, waits for them, and re-layouts, per_device(): blockspec = jnp.stack(blocks, axis=3)  19.1 us
    all_to_all x1, starting transfers between devices, per_device(): lax.all_to_all(series, 'freq', split_axis=1, concat_axis=0, tiled=True)  18.9 us
    dot_general x7, matrix products, per_device(): jnp.dot(flat_table, block_rows, preferred_element_type=jnp.float32)  14.3 us
    unnamed x21, local copies, waits for them, and re-layouts  13.2 us
    all_to_all x2, local copies, waits for them, and re-layouts, per_device(): lax.all_to_all(blockspec, 'freq', split_axis=0, concat_axis=4, tiled=True)  7.57 us
  transfers between devices with their start and end apart: 1, of which 1 were waited for; matrix products, arithmetic and copies ran while one was open for 2% of the time, Pallas kernels for 0%

commit v1 on v0

--- a/solution.py
+++ b/solution.py
@@ -51,7 +51,7 @@
     )
     gram_part = split_quadrants(products, order)[None]
     own_spectra = received[:, :, HALF]
-    gram = lax.psum(gram_part, "space") / total_cells
+    gram = jnp.sum(lax.all_gather(gram_part, "space"), axis=0) / total_cells
     return (own_spectra, gram)
 
 

time: 364 us -> 359 us (0.986)
  blocking collectives: 228 us -> 223 us
    psum x1 -> x0, blocking collectives: 34.6 us -> none  [per_device(): gram = lax.psum(gram_part, 'space') / total_cells]
    all_gather x0 -> x1, blocking collectives: none -> 29.4 us  [per_device(): gram = jnp.sum(lax.all_gather(gram_part, 'space'), axis=0) / total_cells]
where the time goes in v1:
time: 359 us; the launch traced here: 358 us
  blocking collectives  223 us (62%)
  local copies, waits for them, and re-layouts  45.3 us (13%)
  waiting for transfers between devices  33.4 us (9%)
  starting transfers between devices  18.9 us (5%)
  matrix products  15.6 us (4%)
  between operations  15.1 us (4%)
  other arithmetic  6.4 us (2%)
    all_to_all x1, blocking collectives, per_device(): lax.all_to_all(blockspec, 'freq', split_axis=0, concat_axis=4, tiled=True)  193 us
    all_to_all x1, waiting for transfers between devices, per_device(): lax.all_to_all(series, 'freq', split_axis=1, concat_axis=0, tiled=True)  33.4 us
    all_gather x1, blocking collectives, per_device(): gram = jnp.sum(lax.all_gather(gram_part, 'space'), axis=0) / total_cells  29.4 us
    another operation x9, local copies, waits for them, and re-layouts, per_device(): blockspec = jnp.stack(blocks, axis=3)  19.1 us
    all_to_all x1, starting transfers between devices, per_device(): lax.all_to_all(series, 'freq', split_axis=1, concat_axis=0, tiled=True)  18.9 us
    dot_general x7, matrix products, per_device(): jnp.dot(flat_table, block_rows, preferred_element_type=jnp.float32)  14.3 us
    unnamed x21, local copies, waits for them, and re-layouts  13.2 us
    all_to_all x2, local copies, waits for them, and re-layouts, per_device(): lax.all_to_all(blockspec, 'freq', split_axis=0, concat_axis=4, tiled=True)  7.57 us
  transfers between devices with their start and end apart: 1, of which 1 were waited for; matrix products, arithmetic and copies ran while one was open for 2% of the time, Pallas kernels for 0%

profile of v1, /device:TPU:4, one launch (start us, length us, event | category | flops | bytes accessed | tf_op | source)
XLA Modules:
  0.0 357.6 jit_solution(498715291686584251)
XLA Ops:
  0.6 2.3 copy.26
  3.0 18.9 %all-to-all-start = ((bf16[32,64,256]{2,0,1:T(8,128)(2,1)}), bf16[32,64,256]{2,0,1:T(8,128)(2,1)}, u32[]{:S(2)}, u32[]{:S(2)}) async-start(bf16[32,64,256]{2,0,1:T(8,128)(2,1)} %bitcast.41), calls=%async_computation | async-start | bytes 2097152 | tf_op jit(solution)/shard_map/all_to_all | solution.py:38
  33.3 5.4 %multiply_convert_fusion = (bf16[64,1,9,512]{3,0,2,1:T(8,128)(2,1)S(1)}, bf16[64,1,9,512]{3,0,2,1:T(8,128)(2,1)S(1)}) fusion(s32[64,9]{0,1:T(8,128)S(1)} %add_select_fusion.2, f32[512]{0:T(512)S(1)} %fusion.16), kind=kLoop, calls=%fused_computation.15 | loop fusion | flops 5603328 | bytes 1184000 | tf_op jit(solution)/shard_map/convert
  44.5 33.4 %all-to-all-done = bf16[32,64,256]{2,0,1:T(8,128)(2,1)} async-done(((bf16[32,64,256]{2,0,1:T(8,128)(2,1)}), bf16[32,64,256]{2,0,1:T(8,128)(2,1)}, u32[]{:S(2)}, u32[]{:S(2)}) %all-to-all-start) | async-done | bytes 1048608 | tf_op jit(solution)/shard_map/all_to_all | solution.py:38
  77.9 1.5 convolution_convert_fusion.6
  80.6 1.5 convolution_convert_fusion.5
  82.3 2.3 convolution_convert_fusion.4
  84.7 1.3 stack_reshape.23
  86.0 2.3 convolution_convert_fusion.3
  88.3 2.2 stack_reshape.24
  90.5 2.3 convolution_convert_fusion.2
  92.8 2.1 stack_reshape.25
  94.9 2.3 convolution_convert_fusion.1
  97.2 2.1 stack_reshape.26
  99.3 2.3 convolution_convert_fusion
  101.6 1.3 stack_reshape.27
  102.9 1.1 constant_dynamic-update-slice_fusion.5
  110.9 8.5 %copy.18 = bf16[64,2,9,7,256]{4,1,3,2,0:T(2,128)(2,1)} copy(bf16[64,2,9,7,256]{4,2,1,0,3:T(8,128)(2,1)} %constant_dynamic-update-slice_fusion) | data formatting | bytes 8257536 | tf_op jit(solution)/shard_map/stack | solution.py:46
  119.4 193.4 %all_to_all.37 = bf16[64,2,9,7,256]{4,1,3,2,0:T(2,128)(2,1)S(1)} all-to-all(bf16[64,2,9,7,256]{4,1,3,2,0:T(2,128)(2,1)} %copy.18), channel_id=1, replica_groups=mesh['freq'=64,'space'=8] {'freq'}, dimensions={0} | all-to-all | bytes 8257536 | tf_op jit(solution)/shard_map/all_to_all | solution.py:47
  315.3 2.9 copy.24
  318.2 1.2 fusion.25
  319.6 29.4 %all-gather = f32[16,63,63]{2,1,0:T(8,128)S(1)} all-gather(f32[2,63,63]{2,1,0:T(8,128)S(1)} %pad_maximum_fusion.1), channel_id=2, replica_groups=mesh['freq'=64,'space'=8] {'space'}, dimensions={0}, use_global_device_ids=true | all-gather | bytes 285768 | tf_op jit(solution)/shard_map/all_gather | solution.py:54
  349.8 6.7 %copy.23 = bf16[1,64,9,7,1,2,256]{6,5,1,4,3,2,0:T(2,128)(2,1)S(1)} copy(bf16[1,64,9,7,1,2,256]{6,5,4,3,2,1,0:T(2,128)(2,1)} %bitcast.45) | data formatting | bytes 8257536 | tf_op jit(solution)/shard_map/all_to_all | solution.py:47
  356.5 1.1 slice_bitcast_fusion
  (35 shorter events, 14.6 us)
Async XLA Ops:
  3.0 18.9 %copy-start.4 = (s32[7]{0:T(128)S(1)}, s32[7]{0:T(128)}, u32[]{:S(2)}) copy-start(s32[7]{0:T(128)} %param.5) | copy-start | bytes 88
  3.0 30.3 %copy-start.5 = (s32[64]{0:T(128)S(1)}, s32[64]{0:T(128)}, u32[]{:S(2)}) copy-start(s32[64]{0:T(128)} %param.6) | copy-start | bytes 772
  3.0 74.9 %all-to-all-start = ((bf16[32,64,256]{2,0,1:T(8,128)(2,1)}), bf16[32,64,256]{2,0,1:T(8,128)(2,1)}, u32[]{:S(2)}, u32[]{:S(2)}) async-start(bf16[32,64,256]{2,0,1:T(8,128)(2,1)} %bitcast.41), calls=%async_computation | async-start | bytes 2097152 | tf_op jit(solution)/shard_map/all_to_all | solution.py:38
  104.0 1.6 copy-start.1
  105.6 1.6 copy-start.2
  107.2 1.6 copy-start.3
  312.8 1.9 copy-start
